TPU v7x, 32 devices: a whole 2x2x4 slice. The times are simulated.
32 devices in a mesh: grp: 8 (over z, core), rep: 4 (over y, x).
Axes of the slice: x: 2, y: 2, z: 4, core: 2. Of those that a mesh axis runs over, the one named last changes fastest.
Arguments:
- queries: bfloat16 [12288, 2560], P(('grp', 'rep')), may hold values from -60 to 60
- passages: bfloat16 [65536, 2560], P(('grp', 'rep')), may hold values from -60 to 60
- block_valid_counts: int32 [512], P(('grp', 'rep')), may hold values from 16 to 128
- positive_index: int32 [12288], P(('grp', 'rep')), may hold values from 0 to 2047, as said below
- neg_blocks: int32 [32, 12], P(('grp', 'rep')), may hold values from 0 to 511, as said below
- query_weights: float32 [12288], P(('grp', 'rep')), may hold values from 0.3 to 10
Outputs:
- query_loss: float32 [12288], P(('grp', 'rep'))
- mean_loss: float32 [], replicated
Inputs may be any that keep to these rules, and one draw needn't show every extreme that they name: `neg_blocks`: row g lists 12 distinct blocks, all owned by query groups with the same rep index as group g and another grp index; at most 2 of them belong to one group, and some group gives exactly 2 in every row. `positive_index`: always a valid row of one of the query's own group's blocks.
All inputs are finite; a program needn't handle non-finite values.
Results may differ from a plain program's by a relative error of at most 0.0003.
Values may be sent and summed in bfloat16 or wider, within the bound.
A program may use at most 256 MiB of HBM per device.

v0:
```python
import jax
import jax.numpy as jnp
from jax import lax
from jax.sharding import PartitionSpec as P

CAP = 2
inverse_softmax_sharpness = 20.0
norm_epsilon = 1e-06


def normalize(rows):
    values = rows.astype(jnp.float32)
    scale = lax.rsqrt(jnp.sum(values * values, axis=-1, keepdims=True) + norm_epsilon)
    return (values * scale).astype(jnp.bfloat16)


def local(queries, passages, block_valid_counts, positive_index, neg_blocks, query_weights):
    group_count = lax.axis_size("grp")
    replica_count = lax.axis_size("rep")
    local_rows = passages.shape[0]
    blocks_here = block_valid_counts.shape[0]
    block_rows = local_rows // blocks_here
    feature_width = passages.shape[1]
    question_unit_vectors = normalize(queries)
    document_unit_vectors = normalize(passages)
    row_valid = jnp.arange(local_rows, dtype=jnp.int32) % block_rows < jnp.repeat(
        block_valid_counts, block_rows
    )
    shared_pool_similarity = (
        lax.dot_general(
            question_unit_vectors,
            document_unit_vectors,
            (((1,), (1,)), ((), ())),
            preferred_element_type=jnp.float32,
        )
        * inverse_softmax_sharpness
    )
    local_total = jnp.sum(
        jnp.where(row_valid[None, :], jnp.exp(shared_pool_similarity), 0.0), axis=1
    )
    positive_score = jnp.take_along_axis(shared_pool_similarity, positive_index[:, None], axis=1)[
        :, 0
    ]
    wanted = neg_blocks[0]
    owner_device = wanted // blocks_here
    owner_group = owner_device // replica_count
    local_block = wanted % blocks_here
    listed = wanted.shape[0]
    same_owner = owner_group[:, None] == owner_group[None, :]
    earlier_slot = jnp.arange(listed)[:, None] > jnp.arange(listed)[None, :]
    slot_rank = jnp.sum(jnp.logical_and(same_owner, earlier_slot), axis=1)
    requests = (
        jnp.full((group_count, CAP), -1, jnp.int32).at[owner_group, slot_rank].set(local_block)
    )
    incoming = lax.all_to_all(requests, "grp", split_axis=0, concat_axis=0, tiled=True)
    requested = incoming >= 0
    safe_block = jnp.maximum(incoming, 0)
    matches = safe_block[:, :, None] == jnp.arange(blocks_here, dtype=jnp.int32)[None, None, :]
    slot_counts = jnp.where(
        requested, jnp.sum(jnp.where(matches, block_valid_counts[None, None, :], 0), axis=2), 0
    )
    unit_blocks = document_unit_vectors.reshape(blocks_here, block_rows, feature_width)
    picked = unit_blocks[safe_block]
    arrived = lax.all_to_all(picked, "grp", split_axis=0, concat_axis=0, tiled=True)
    kept_counts = lax.all_to_all(slot_counts, "grp", split_axis=0, concat_axis=0, tiled=True)
    similarity = (
        jnp.einsum(
            "qd,skrd->kqsr", question_unit_vectors, arrived, preferred_element_type=jnp.float32
        )
        * inverse_softmax_sharpness
    )
    live_rows = jnp.arange(block_rows, dtype=jnp.int32)[None, None, :] < kept_counts[:, :, None]
    live_rows = jnp.transpose(live_rows, (1, 0, 2))[:, None]
    slot_totals = jnp.sum(jnp.where(live_rows, jnp.exp(similarity), 0.0), axis=(2, 3))
    hard_total = jnp.sum(slot_totals, axis=0)
    query_loss = jnp.log(local_total + hard_total) - positive_score
    weighted_sum, weight_sum = lax.psum(
        (jnp.sum(query_weights * query_loss), jnp.sum(query_weights)), ("grp", "rep")
    )
    return (query_loss, weighted_sum / weight_sum)


def solution(mesh):
    in_specs = (
        P(("grp", "rep"), None),
        P(("grp", "rep"), None),
        P(("grp", "rep")),
        P(("grp", "rep")),
        P(("grp", "rep"), None),
        P(("grp", "rep")),
    )
    out_specs = (P(("grp", "rep")), P())
    return jax.shard_map(local, mesh=mesh, in_specs=in_specs, out_specs=out_specs, check_vma=False)
```

profile of v0, /device:TPU:12, one launch (start us, length us, event | category | flops | bytes accessed | tf_op | source)
XLA Modules:
  0.0 324.3 jit_solution(4056627843211229691)
XLA Ops:
  0.6 0.7 fusion.21
  1.3 0.7 and_select_fusion
  2.0 0.2 convert_reduce_fusion
  2.2 0.7 fusion.22
  2.8 1.1 scatter_fusion
  4.0 0.7 copy.22
  4.6 5.3 %all-to-all-start = ((s32[8,1,2]{2,1,0:T(1,128)}), s32[8,1,2]{2,1,0:T(1,128)S(1)}, u32[]{:S(2)}, u32[]{:S(2)}) async-start(s32[8,1,2]{2,1,0:T(1,128)} %copy.22), calls=%async_computation | async-start | bytes 8192 | tf_op jit(solution)/shard_map/all_to_all | solution.py:55
  10.0 6.2 %fusion = f32[2048]{0:T(1024)S(1)} fusion(bf16[2048,2560]{1,0:T(8,128)(2,1)} %param.7), kind=kLoop, calls=%fused_computation.5 | loop fusion | flops 15726592 | bytes 10493952 | tf_op jit(solution)/shard_map/reduce_sum | solution.py:13
  16.2 0.7 copy-done
  16.9 5.5 %fusion.1 = bf16[2048,2560]{1,0:T(8,128)(2,1)} fusion(bf16[2048,2560]{1,0:T(8,128)(2,1)S(1)} %copy-done, f32[2048]{0:T(1024)S(1)} %add_rsqrt_fusion), kind=kLoop, calls=%fused_computation.6 | loop fusion | flops 15728640 | bytes 20979712 | tf_op jit(solution)/shard_map/convert_element_type | solution.py:14
  22.4 0.0 all-to-all-done
  22.4 0.1 copy.23
  22.5 0.2 select_reduce_fusion.1
  22.7 0.7 copy.25
  23.4 0.1 copy.28
  23.5 0.1 reshape.238
  23.6 5.1 %all-to-all-start.1 = ((s32[8,1,2]{2,1,0:T(1,128)}), s32[8,1,2]{2,1,0:T(1,128)S(1)}, u32[]{:S(2)}, u32[]{:S(2)}) async-start(s32[8,1,2]{2,1,0:T(1,128)} %copy.25), calls=%async_computation.1 | async-start | bytes 8192 | tf_op jit(solution)/shard_map/all_to_all | solution.py:65
  28.7 9.6 %gather_fusion = bf16[16,128,2560]{2,1,0:T(8,128)(2,1)} fusion(bf16[16,128,2560]{2,1,0:T(8,128)(2,1)} %bitcast.68, s32[1024]{0:T(1024)S(1)} %pad_clamp_fusion), kind=kCustom, calls=%fused_computation | custom fusion | bytes 20971584 | tf_op jit(solution)/shard_map/gather | solution.py:63
  38.2 0.0 all-to-all-done.1
  38.3 5.2 %all-to-all-start.2 = ((bf16[8,2,128,2560]{3,2,1,0:T(8,128)(2,1)}), bf16[8,2,128,2560]{3,2,1,0:T(8,128)(2,1)}, u32[]{:S(2)}, u32[]{:S(2)}) async-start(bf16[8,2,128,2560]{3,2,1,0:T(8,128)(2,1)} %bitcast.69), calls=%async_computation.2 | async-start | bytes 20971520 | tf_op jit(solution)/shard_map/all_to_all | solution.py:64
  43.6 0.1 fusion.11
  43.7 0.5 fusion.2
  44.1 9.9 %select_reduce_fusion = (f32[384]{0:T(512)S(1)}, f32[384,2048]{1,0:T(8,128)}) fusion(pred[2048]{0:T(1024)(128)(4,1)S(1)} %fusion.11, bf16[2048,2560]{1,0:T(8,128)(2,1)} %fusion.1, bf16[384,2560]{1,0:T(8,128)(2,1)S(1)} %copy-done.1, f32[384]{0:T(512)S(1)} %add_rsqrt_fusion.1), kind=kOutput, calls=%fused_computation.13 | convolution fusion | flops 4031839744 | bytes 15602688 | tf_op jit(solution)/shard_map/dot_general | solution.py:30
  54.0 5.2 %gather_fusion.1 = f32[384]{0:T(512)S(1)} fusion(f32[384,2048]{1,0:T(8,128)} %get-tuple-element.12, s32[384]{0:T(512)S(1)} %fusion.19), kind=kCustom, calls=%fused_computation.1 | custom fusion | bytes 6144 | tf_op jit(solution)/shard_map/jit(take_along_axis)/gather | solution.py:41
  59.2 0.1 copy.26
  59.3 0.1 copy.27
  59.4 0.1 iota_compare_fusion.2
  59.4 0.0 copy-start.4
  59.5 209.4 %all-to-all-done.2 = bf16[8,2,128,2560]{3,2,1,0:T(8,128)(2,1)} async-done(((bf16[8,2,128,2560]{3,2,1,0:T(8,128)(2,1)}), bf16[8,2,128,2560]{3,2,1,0:T(8,128)(2,1)}, u32[]{:S(2)}, u32[]{:S(2)}) %all-to-all-start.2) | async-done | bytes 10485792 | tf_op jit(solution)/shard_map/all_to_all | solution.py:64
  268.8 8.5 %fusion.4 = f32[384]{0:T(512)S(1)} fusion(pred[2,8,128]{2,0,1:T(4,128)(4,1)S(1)} %iota_compare_fusion.2, bf16[8,2,128,2560]{3,2,1,0:T(8,128)(2,1)} %all-to-all-done.2, bf16[384,2560]{1,0:T(8,128)(2,1)S(1)} %copy-done.1, f32[384]{0:T(512)S(1)} %add_rsqrt_fusion.1), kind=kOutput, calls=%fused_computation.12 | convolution fusion | flops 4031839744 | bytes 12456960 | tf_op jit(solution)/shard_map/qd,skrd->kqsr/dot_general | solution.py:67
  277.3 1.3 fusion.24
  278.6 43.4 %all-reduce = (f32[]{:T(128)}, f32[]{:T(128)}) all-reduce(f32[]{:T(128)} %get-tuple-element.3, f32[]{:T(128)} %get-tuple-element.2), channel_id=1, replica_groups=mesh['grp'=8,'rep'=4] {'grp','rep'}, use_global_device_ids=true, to_apply=%region_8.9 | all-reduce | flops 2 | bytes 16 | tf_op jit(solution)/shard_map/psum | solution.py:77
  (19 shorter events, 0.1 us)
Async XLA Ops:
  4.6 17.8 %all-to-all-start = ((s32[8,1,2]{2,1,0:T(1,128)}), s32[8,1,2]{2,1,0:T(1,128)S(1)}, u32[]{:S(2)}, u32[]{:S(2)}) async-start(s32[8,1,2]{2,1,0:T(1,128)} %copy.22), calls=%async_computation | async-start | bytes 8192 | tf_op jit(solution)/shard_map/all_to_all | solution.py:55
  10.0 7.0 %copy-start = (bf16[2048,2560]{1,0:T(8,128)(2,1)S(1)}, bf16[2048,2560]{1,0:T(8,128)(2,1)}, u32[]{:S(2)}) copy-start(bf16[2048,2560]{1,0:T(8,128)(2,1)} %param.7) | copy-start | bytes 31457284
  16.9 5.6 %copy-start.3 = (s32[16]{0:T(128)S(1)}, s32[16]{0:T(128)}, u32[]{:S(2)}) copy-start(s32[16]{0:T(128)} %param.8) | copy-start | bytes 196
  23.6 14.7 %all-to-all-start.1 = ((s32[8,1,2]{2,1,0:T(1,128)}), s32[8,1,2]{2,1,0:T(1,128)S(1)}, u32[]{:S(2)}, u32[]{:S(2)}) async-start(s32[8,1,2]{2,1,0:T(1,128)} %copy.25), calls=%async_computation.1 | async-start | bytes 8192 | tf_op jit(solution)/shard_map/all_to_all | solution.py:65
  38.2 5.2 %copy-start.2 = (s32[384]{0:T(512)S(1)}, s32[384]{0:T(512)}, u32[]{:S(2)}) copy-start(s32[384]{0:T(512)} %param.9) | copy-start | bytes 4612
  38.3 5.4 %copy-start.1 = (bf16[384,2560]{1,0:T(8,128)(2,1)S(1)}, bf16[384,2560]{1,0:T(8,128)(2,1)}, u32[]{:S(2)}) copy-start(bf16[384,2560]{1,0:T(8,128)(2,1)} %param.6) | copy-start | bytes 5898244
  38.3 230.6 %all-to-all-start.2 = ((bf16[8,2,128,2560]{3,2,1,0:T(8,128)(2,1)}), bf16[8,2,128,2560]{3,2,1,0:T(8,128)(2,1)}, u32[]{:S(2)}, u32[]{:S(2)}) async-start(bf16[8,2,128,2560]{3,2,1,0:T(8,128)(2,1)} %bitcast.69), calls=%async_computation.2 | async-start | bytes 20971520 | tf_op jit(solution)/shard_map/all_to_all | solution.py:64
  59.4 217.9 %copy-start.4 = (f32[384]{0:T(512)S(1)}, f32[384]{0:T(512)}, u32[]{:S(2)}) copy-start(f32[384]{0:T(512)} %param.11) | copy-start | bytes 4612
where the time goes:
time: 325 us; the launch traced here: 324 us
  waiting for transfers between devices  209 us (64%)
  blocking collectives  43.4 us (13%)
  matrix products  18.4 us (6%)
  local copies, waits for them, and re-layouts  18.3 us (6%)
  other arithmetic  16.1 us (5%)
  starting transfers between devices  15.7 us (5%)
    all_to_all x1, waiting for transfers between devices, local(): lax.all_to_all(picked, 'grp', split_axis=0, concat_axis=0, tiled=True)  209 us
    psum x1, blocking collectives, local(): lax.psum((jnp.sum(query_weights * query_loss), jnp.sum(query_weights)), (...  43.4 us
    dot_general x1, matrix products, local(): lax.dot_general(question_unit_vectors, document_unit_vectors, (((1,), (1,...  9.91 us
    gather x1, local copies, waits for them, and re-layouts, local(): picked = unit_blocks[safe_block]  9.57 us
    dot_general x1, matrix products, local(): jnp.einsum('qd,skrd->kqsr', question_unit_vectors, arrived, preferred_ele...  8.48 us
    reduce_sum x2, other arithmetic, normalize(): jnp.sum(values * values, axis=-1, keepdims=True) + norm_epsilon  6.69 us
  transfers between devices with their start and end apart: 3, of which 1 were waited for; matrix products, arithmetic and copies ran while one was open for 11% of the time, Pallas kernels for 0%

commit v1 on v0

--- a/solution.py
+++ b/solution.py
@@ -75,7 +75,7 @@
     hard_total = jnp.sum(slot_totals, axis=0)
     query_loss = jnp.log(local_total + hard_total) - positive_score
     weighted_sum, weight_sum = lax.psum(
-        (jnp.sum(query_weights * query_loss), jnp.sum(query_weights)), ("grp", "rep")
+        lax.psum((jnp.sum(query_weights * query_loss), jnp.sum(query_weights)), "rep"), "grp"
     )
     return (query_loss, weighted_sum / weight_sum)
 

time: 325 us -> 311 us (0.957)
  the two profiles are of different devices: /device:TPU:12 before, /device:TPU:0 now
where the time goes in v1:
time: 311 us; the launch traced here: 310 us
  waiting for transfers between devices  213 us (68%)
  blocking collectives  24.8 us (8%)
  local copies, waits for them, and re-layouts  18.4 us (6%)
  matrix products  18.4 us (6%)
  starting transfers between devices  16.7 us (5%)
  other arithmetic  16 us (5%)
  between operations  3.13 us (1%)
    all_to_all x1, waiting for transfers between devices, local(): lax.all_to_all(picked, 'grp', split_axis=0, concat_axis=0, tiled=True)  213 us
    psum x1, blocking collectives, local(): lax.psum(lax.psum((jnp.sum(query_weights * query_loss), jnp.sum(query_wei...  14.2 us
    psum x1, blocking collectives, local(): lax.psum((jnp.sum(query_weights * query_loss), jnp.sum(query_weights)), '...  10.6 us
    dot_general x1, matrix products, local(): lax.dot_general(question_unit_vectors, document_unit_vectors, (((1,), (1,...  9.91 us
    gather x1, local copies, waits for them, and re-layouts, local(): picked = unit_blocks[safe_block]  9.57 us
    dot_general x1, matrix products, local(): jnp.einsum('qd,skrd->kqsr', question_unit_vectors, arrived, preferred_ele...  8.48 us
    reduce_sum x2, other arithmetic, normalize(): jnp.sum(values * values, axis=-1, keepdims=True) + norm_epsilon  6.69 us
    all_to_all x1, starting transfers between devices, local(): lax.all_to_all(requests, 'grp', split_axis=0, concat_axis=0, tiled=True)  6.35 us
  transfers between devices with their start and end apart: 3, of which 1 were waited for; matrix products, arithmetic and copies ran while one was open for 12% of the time, Pallas kernels for 0%

profile of v1, /device:TPU:0, one launch (start us, length us, event | category | flops | bytes accessed | tf_op | source)
XLA Modules:
  0.0 310.3 jit_solution(13518792082319401792)
XLA Ops:
  0.6 0.7 fusion.21
  1.3 0.7 and_select_fusion
  2.0 0.2 convert_reduce_fusion
  2.2 0.7 fusion.22
  2.8 1.1 scatter_fusion
  4.0 0.7 copy.22
  4.6 6.4 %all-to-all-start = ((s32[8,1,2]{2,1,0:T(1,128)}), s32[8,1,2]{2,1,0:T(1,128)S(1)}, u32[]{:S(2)}, u32[]{:S(2)}) async-start(s32[8,1,2]{2,1,0:T(1,128)} %copy.22), calls=%async_computation | async-start | bytes 8192 | tf_op jit(solution)/shard_map/all_to_all | solution.py:55
  11.0 6.2 %fusion = f32[2048]{0:T(1024)S(1)} fusion(bf16[2048,2560]{1,0:T(8,128)(2,1)} %param.7), kind=kLoop, calls=%fused_computation.5 | loop fusion | flops 15726592 | bytes 10493952 | tf_op jit(solution)/shard_map/reduce_sum | solution.py:13
  17.2 0.7 copy-done
  17.9 5.5 %fusion.1 = bf16[2048,2560]{1,0:T(8,128)(2,1)} fusion(bf16[2048,2560]{1,0:T(8,128)(2,1)S(1)} %copy-done, f32[2048]{0:T(1024)S(1)} %add_rsqrt_fusion), kind=kLoop, calls=%fused_computation.6 | loop fusion | flops 15728640 | bytes 20979712 | tf_op jit(solution)/shard_map/convert_element_type | solution.py:14
  23.4 0.0 all-to-all-done
  23.4 0.1 copy.23
  23.5 0.2 select_reduce_fusion.1
  23.8 0.7 copy.25
  24.4 0.1 copy.28
  24.5 0.1 reshape.238
  24.6 5.1 %all-to-all-start.1 = ((s32[8,1,2]{2,1,0:T(1,128)}), s32[8,1,2]{2,1,0:T(1,128)S(1)}, u32[]{:S(2)}, u32[]{:S(2)}) async-start(s32[8,1,2]{2,1,0:T(1,128)} %copy.25), calls=%async_computation.1 | async-start | bytes 8192 | tf_op jit(solution)/shard_map/all_to_all | solution.py:65
  29.7 9.6 %gather_fusion = bf16[16,128,2560]{2,1,0:T(8,128)(2,1)} fusion(bf16[16,128,2560]{2,1,0:T(8,128)(2,1)} %bitcast.68, s32[1024]{0:T(1024)S(1)} %pad_clamp_fusion), kind=kCustom, calls=%fused_computation | custom fusion | bytes 20971584 | tf_op jit(solution)/shard_map/gather | solution.py:63
  39.3 0.0 all-to-all-done.1
  39.3 5.3 %all-to-all-start.2 = ((bf16[8,2,128,2560]{3,2,1,0:T(8,128)(2,1)}), bf16[8,2,128,2560]{3,2,1,0:T(8,128)(2,1)}, u32[]{:S(2)}, u32[]{:S(2)}) async-start(bf16[8,2,128,2560]{3,2,1,0:T(8,128)(2,1)} %bitcast.69), calls=%async_computation.2 | async-start | bytes 20971520 | tf_op jit(solution)/shard_map/all_to_all | solution.py:64
  44.7 0.1 fusion.11
  44.7 0.5 fusion.2
  45.2 9.9 %select_reduce_fusion = (f32[384]{0:T(512)S(1)}, f32[384,2048]{1,0:T(8,128)}) fusion(pred[2048]{0:T(1024)(128)(4,1)S(1)} %fusion.11, bf16[2048,2560]{1,0:T(8,128)(2,1)} %fusion.1, bf16[384,2560]{1,0:T(8,128)(2,1)S(1)} %copy-done.1, f32[384]{0:T(512)S(1)} %add_rsqrt_fusion.1), kind=kOutput, calls=%fused_computation.13 | convolution fusion | flops 4031839744 | bytes 15602688 | tf_op jit(solution)/shard_map/dot_general | solution.py:30
  55.1 5.2 %gather_fusion.1 = f32[384]{0:T(512)S(1)} fusion(f32[384,2048]{1,0:T(8,128)} %get-tuple-element.14, s32[384]{0:T(512)S(1)} %fusion.19), kind=kCustom, calls=%fused_computation.1 | custom fusion | bytes 6144 | tf_op jit(solution)/shard_map/jit(take_along_axis)/gather | solution.py:41
  60.3 0.1 copy.26
  60.4 0.1 copy.27
  60.5 0.1 iota_compare_fusion.2
  60.6 212.8 %all-to-all-done.2 = bf16[8,2,128,2560]{3,2,1,0:T(8,128)(2,1)} async-done(((bf16[8,2,128,2560]{3,2,1,0:T(8,128)(2,1)}), bf16[8,2,128,2560]{3,2,1,0:T(8,128)(2,1)}, u32[]{:S(2)}, u32[]{:S(2)}) %all-to-all-start.2) | async-done | bytes 10485792 | tf_op jit(solution)/shard_map/all_to_all | solution.py:64
  273.4 8.5 %fusion.4 = f32[384]{0:T(512)S(1)} fusion(pred[2,8,128]{2,0,1:T(4,128)(4,1)S(1)} %iota_compare_fusion.2, bf16[8,2,128,2560]{3,2,1,0:T(8,128)(2,1)} %all-to-all-done.2, bf16[384,2560]{1,0:T(8,128)(2,1)S(1)} %copy-done.1, f32[384]{0:T(512)S(1)} %add_rsqrt_fusion.1), kind=kOutput, calls=%fused_computation.12 | convolution fusion | flops 4031839744 | bytes 12456960 | tf_op jit(solution)/shard_map/qd,skrd->kqsr/dot_general | solution.py:67
  281.9 1.2 fusion.24
  283.1 10.6 %all-reduce.1 = (f32[]{:T(128)}, f32[]{:T(128)}) all-reduce(f32[]{:T(128)} %get-tuple-element.3, f32[]{:T(128)} %get-tuple-element.2), channel_id=1, replica_groups=mesh['grp'=8,'rep'=4] {'rep'}, use_global_device_ids=true, to_apply=%region_8.9 | all-reduce | flops 2 | bytes 16 | tf_op jit(solution)/shard_map/psum | solution.py:78
  293.7 14.2 %all-reduce = (f32[]{:T(128)}, f32[]{:T(128)}) all-reduce(f32[]{:T(128)} %get-tuple-element.6, f32[]{:T(128)} %get-tuple-element.7), channel_id=1, replica_groups=mesh['grp'=8,'rep'=4] {'grp'}, use_global_device_ids=true, to_apply=%region_9.10 | all-reduce | flops 2 | bytes 16 | tf_op jit(solution)/shard_map/psum | solution.py:77
  (20 shorter events, 0.1 us)
Async XLA Ops:
  4.6 18.8 %all-to-all-start = ((s32[8,1,2]{2,1,0:T(1,128)}), s32[8,1,2]{2,1,0:T(1,128)S(1)}, u32[]{:S(2)}, u32[]{:S(2)}) async-start(s32[8,1,2]{2,1,0:T(1,128)} %copy.22), calls=%async_computation | async-start | bytes 8192 | tf_op jit(solution)/shard_map/all_to_all | solution.py:55
  11.0 7.0 %copy-start = (bf16[2048,2560]{1,0:T(8,128)(2,1)S(1)}, bf16[2048,2560]{1,0:T(8,128)(2,1)}, u32[]{:S(2)}) copy-start(bf16[2048,2560]{1,0:T(8,128)(2,1)} %param.7) | copy-start | bytes 31457284
  17.9 5.6 %copy-start.3 = (s32[16]{0:T(128)S(1)}, s32[16]{0:T(128)}, u32[]{:S(2)}) copy-start(s32[16]{0:T(128)} %param.8) | copy-start | bytes 196
  24.6 14.7 %all-to-all-start.1 = ((s32[8,1,2]{2,1,0:T(1,128)}), s32[8,1,2]{2,1,0:T(1,128)S(1)}, u32[]{:S(2)}, u32[]{:S(2)}) async-start(s32[8,1,2]{2,1,0:T(1,128)} %copy.25), calls=%async_computation.1 | async-start | bytes 8192 | tf_op jit(solution)/shard_map/all_to_all | solution.py:65
  39.3 5.3 %copy-start.2 = (s32[384]{0:T(512)S(1)}, s32[384]{0:T(512)}, u32[]{:S(2)}) copy-start(s32[384]{0:T(512)} %param.9) | copy-start | bytes 4612
  39.3 5.5 %copy-start.1 = (bf16[384,2560]{1,0:T(8,128)(2,1)S(1)}, bf16[384,2560]{1,0:T(8,128)(2,1)}, u32[]{:S(2)}) copy-start(bf16[384,2560]{1,0:T(8,128)(2,1)} %param.6) | copy-start | bytes 5898244
  39.3 234.1 %all-to-all-start.2 = ((bf16[8,2,128,2560]{3,2,1,0:T(8,128)(2,1)}), bf16[8,2,128,2560]{3,2,1,0:T(8,128)(2,1)}, u32[]{:S(2)}, u32[]{:S(2)}) async-start(bf16[8,2,128,2560]{3,2,1,0:T(8,128)(2,1)} %bitcast.69), calls=%async_computation.2 | async-start | bytes 20971520 | tf_op jit(solution)/shard_map/all_to_all | solution.py:64
  60.6 221.3 %copy-start.4 = (f32[384]{0:T(512)S(1)}, f32[384]{0:T(512)}, u32[]{:S(2)}) copy-start(f32[384]{0:T(512)} %param.11) | copy-start | bytes 4612
